TPU v7x, 32 devices: a whole 2x2x4 slice. The times are simulated.
32 devices in a mesh: grp: 2 (over core), kv: 2 (over x), srv: 8 (over z, y).
Axes of the slice: x: 2, y: 2, z: 4, core: 2. Of those that a mesh axis runs over, the one named last changes fastest.
Arguments:
- queries: bfloat16 [2048, 8, 1024], P('srv', 'kv', 'grp'), may hold values from -120 to 120
- keys: bfloat16 [2048, 8, 128], P('srv', 'kv'), may hold values from -5 to 5
- values: bfloat16 [2048, 8, 128], P('srv', 'kv'), may hold values from -6 to 6
- lengths: int32 [4], replicated, may hold values from 1 to 1024, 2048 in all
- output_projection_weight: bfloat16 [8, 1024, 8192], P('kv', 'grp', 'srv'), may hold values from -0.0625 to 0.0625
Outputs:
- projected: bfloat16 [2048, 8192], P('srv', ('grp', 'kv'))
Inputs may be any that keep to these rules, and one draw needn't show every extreme that they name: The 4 lengths sum to 2048; the longest document has exactly 1024 tokens.
All inputs are finite; a program needn't handle non-finite values.
Results may differ from a plain program's by a relative error of at most 0.017.
Values may be sent and summed in bfloat16 or wider, within the bound.
A program may use at most 128 MiB of HBM per device.

v0:
```python
import math

import jax
import jax.numpy as jnp
from jax import lax
from jax.sharding import PartitionSpec as P

REACH = 4


def from_behind(block, axis, distance):
    devices = range(lax.axis_size(axis))
    route = [(i - distance, i) for i in devices if i - distance in devices]
    return lax.ppermute(block, axis, route)


def doc_starts(lengths, position):
    starts = jnp.cumsum(lengths) - lengths
    chosen = jnp.where(starts[None, :] <= position[:, None], starts[None, :], 0)
    return jnp.max(chosen, axis=1)


def attend(queries, window_keys, window_values, query_pos, key_pos, lengths):
    token_count = queries.shape[0]
    groups = queries.shape[1]
    head_size = window_keys.shape[2]
    heads = queries.shape[2] // head_size
    split_output = queries.reshape(token_count, groups, heads, head_size)
    scores = jnp.einsum(
        "tjhd,wjd->jhtw", split_output, window_keys, preferred_element_type=jnp.float32
    )
    scores = scores * (1.0 / math.sqrt(head_size))
    first_key = doc_starts(lengths, query_pos)
    allowed = (key_pos[None, :] >= first_key[:, None]) & (key_pos[None, :] <= query_pos[:, None])
    scores = jnp.where(allowed[None, None], scores, -jnp.inf)
    peak = jnp.max(scores, axis=3, keepdims=True)
    weights = jnp.exp(scores - peak)
    total = jnp.sum(weights, axis=3)
    numer = jnp.einsum(
        "jhtw,wjd->tjhd",
        weights.astype(jnp.bfloat16),
        window_values,
        preferred_element_type=jnp.float32,
    )
    final_output = numer / jnp.transpose(total, (2, 0, 1))[..., None]
    return final_output.astype(jnp.bfloat16).reshape(token_count, groups * heads * head_size)


def on_device(queries, keys, values, lengths, output_projection_weight):
    token_count = queries.shape[0]
    shard = lax.axis_index("srv")
    stacked = jnp.stack([keys, values])
    arrived = [stacked]
    for distance in range(1, REACH + 1):
        arrived.append(from_behind(stacked, "srv", distance))
    window = jnp.concatenate(arrived[::-1], axis=1)
    query_pos = shard * token_count + jnp.arange(token_count, dtype=jnp.int32)
    key_pos = (shard - REACH) * token_count + jnp.arange(window.shape[1], dtype=jnp.int32)
    attention_output = attend(queries, window[0], window[1], query_pos, key_pos, lengths)
    inner = attention_output.shape[1]
    piece = lax.all_gather(output_projection_weight, "srv", axis=2, tiled=True)
    partial_sum = jnp.dot(
        attention_output, piece.reshape(inner, piece.shape[2]), preferred_element_type=jnp.float32
    )
    summed = lax.psum_scatter(
        partial_sum.astype(jnp.bfloat16), ("grp", "kv"), scatter_dimension=1, tiled=True
    )
    return summed


def solution(mesh):
    placed = (
        P("srv", "kv", "grp"),
        P("srv", "kv", None),
        P("srv", "kv", None),
        P(),
        P("kv", "grp", "srv"),
    )
    return jax.shard_map(
        on_device, mesh=mesh, in_specs=placed, out_specs=P("srv", ("grp", "kv")), check_vma=False
    )
```

profile of v0, /device:TPU:3, one launch (start us, length us, event | category | flops | bytes accessed | tf_op | source)
XLA Modules:
  0.0 737.2 jit_solution(14337410522917652714)
XLA Ops:
  6.5 0.0 all-gather.2.cloned.1.call-start
  6.6 0.7 all-gather.2.cloned.1.call-update
  7.3 0.0 reduce-scatter.2.cloned.1.call-start
  7.3 0.2 copy-done.3
  7.5 0.1 copy-done.2
  7.6 0.1 copy_bitcast_fusion
  7.6 0.1 pad_maximum_fusion
  7.7 5.0 collective-permute-start
  12.7 5.0 collective-permute-start.1
  17.7 2.1 collective-permute-start.2
  19.8 2.8 collective-permute-start.3
  22.6 0.2 reduce-window.9
  22.8 0.1 select_reduce_fusion
  22.9 0.3 compare_and_fusion
  23.2 0.4 reshape.102
  23.7 5.0 collective-permute-done
  28.6 1.1 constant_dynamic-update-slice_fusion.4
  29.7 21.4 %collective-permute-done.1 = bf16[2,256,4,128]{3,1,2,0:T(8,128)(2,1)} collective-permute-done((bf16[2,256,4,128]{3,1,2,0:T(8,128)(2,1)S(1)}, bf16[2,256,4,128]{3,1,2,0:T(8,128)(2,1)}, u32[]{:S(2)}, u32[]{:S(2)}) %collective-permute-start.1) | collective-permute-done | bytes 524320 | tf_op jit(solution)/shard_map/ppermute | solution.py:14
  51.1 1.1 constant_dynamic-update-slice_fusion.3
  52.2 21.4 %collective-permute-done.2 = bf16[2,256,4,128]{3,1,2,0:T(8,128)(2,1)} collective-permute-done((bf16[2,256,4,128]{3,1,2,0:T(8,128)(2,1)S(1)}, bf16[2,256,4,128]{3,1,2,0:T(8,128)(2,1)}, u32[]{:S(2)}, u32[]{:S(2)}) %collective-permute-start.2) | collective-permute-done | bytes 524320 | tf_op jit(solution)/shard_map/ppermute | solution.py:14
  73.6 1.1 constant_dynamic-update-slice_fusion.2
  74.7 32.8 %collective-permute-done.3 = bf16[2,256,4,128]{3,1,2,0:T(8,128)(2,1)} collective-permute-done((bf16[2,256,4,128]{3,1,2,0:T(8,128)(2,1)S(1)}, bf16[2,256,4,128]{3,1,2,0:T(8,128)(2,1)}, u32[]{:S(2)}, u32[]{:S(2)}) %collective-permute-start.3) | collective-permute-done | bytes 524320 | tf_op jit(solution)/shard_map/ppermute | solution.py:14
  107.5 1.1 constant_dynamic-update-slice_fusion.1
  108.6 0.1 constant_dynamic-update-slice_fusion
  108.6 3.1 fusion.9
  111.7 3.0 fusion
  114.8 4.0 copy-done
  118.8 10.4 %fusion.5 = bf16[256,4,4,128]{0,3,2,1:T(8,128)(2,1)S(1)} fusion(f32[4,4,256,1280]{2,3,1,0:T(8,128)} %copy-done, f32[4,4,256]{2,1,0:T(4,128)S(1)} %get-tuple-element.5, bf16[2,1280,4,128]{3,1,2,0:T(8,128)(2,1)S(1)} %constant_dynamic-update-slice_fusion, f32[256,4,4]{0,2,1:T(4,128)S(1)} %bitcast.35), kind=kOutput, calls=%fused_computation.8 | convolution fusion | flops 1353711616 | bytes 23363584 | tf_op jit(solution)/shard_map/jhtw,wjd->tjhd/dot_general | solution.py:39
  129.2 531.9 %all-gather.2.cloned.1.call-done = bf16[4,512,8192]{2,1,0:T(8,128)(2,1)} async-done(((bf16[4,512,1024]{2,1,0:T(8,128)(2,1)}), bf16[4,512,8192]{2,1,0:T(8,128)(2,1)}) %all-gather.2.cloned.1.call-update) | async-done | bytes 33554448 | tf_op jit(solution)/shard_map/all_gather | solution.py:61
  661.1 16.5 %convolution_convert_fusion = bf16[256,8192]{1,0:T(8,128)(2,1)} fusion(bf16[256,2048]{0,1:T(8,128)(2,1)S(1)} %bitcast.34, bf16[2048,8192]{1,0:T(8,128)(2,1)} %bitcast.33), kind=kOutput, calls=%fused_computation.6 | convolution fusion | flops 8592031744 | bytes 38797312 | tf_op jit(solution)/shard_map/dot_general | solution.py:62
  677.6 0.0 reduce-scatter.2.cloned.1.call-update
  677.6 52.7 %reduce-scatter.2.cloned.1.call-done = bf16[256,2048]{1,0:T(8,128)(2,1)} async-done(((bf16[256,8192]{1,0:T(8,128)(2,1)}), bf16[256,2048]{1,0:T(8,128)(2,1)}) %reduce-scatter.2.cloned.1.call-update) | async-done | bytes 1048592 | tf_op jit(solution)/shard_map/reduce_scatter | solution.py:65
  (10 shorter events, 0.0 us)
Async XLA Ops:
  6.5 0.9 copy-start.3
  6.5 1.0 copy-start.2
  6.5 16.1 %copy-start.4 = (s32[4]{0:T(128)S(1)}, s32[4]{0:T(128)}, u32[]{:S(2)}) copy-start(s32[4]{0:T(128)} %param.8) | copy-start | bytes 52
  6.5 16.7 %copy-start.1 = (bf16[256,4,512]{2,1,0:T(4,128)(2,1)S(1)}, bf16[256,4,512]{2,1,0:T(4,128)(2,1)}, u32[]{:S(2)}) copy-start(bf16[256,4,512]{2,1,0:T(4,128)(2,1)} %param.5) | copy-start | bytes 3145732
  6.5 654.5 %all-gather.2.cloned.1.call-start = ((), (), s32[]{:S(2)}) async-start(), calls=%async_computation.1 | async-start | bytes 37748736 | tf_op jit(solution)/shard_map/all_gather | solution.py:61
  7.3 723.1 %reduce-scatter.2.cloned.1.call-start = ((), (), s32[]{:S(2)}) async-start(), calls=%async_computation.2 | async-start | bytes 5242880 | tf_op jit(solution)/shard_map/reduce_scatter | solution.py:65
  7.7 20.9 %collective-permute-start = (bf16[2,256,4,128]{3,1,2,0:T(8,128)(2,1)S(1)}, bf16[2,256,4,128]{3,1,2,0:T(8,128)(2,1)}, u32[]{:S(2)}, u32[]{:S(2)}) collective-permute-start(bf16[2,256,4,128]{3,1,2,0:T(8,128)(2,1)S(1)} %pad_maximum_fusion), channel_id=1, source_target_pairs={{0,4},{1,5},{2,6},{3,7},{8,12},{9,13},{10,14},{11,15},{16,20},{17,... | collective-permute-start | bytes 1572872 | tf_op jit(solution)/shard_map/ppermute | solution.py:14
  12.7 38.4 %collective-permute-start.1 = (bf16[2,256,4,128]{3,1,2,0:T(8,128)(2,1)S(1)}, bf16[2,256,4,128]{3,1,2,0:T(8,128)(2,1)}, u32[]{:S(2)}, u32[]{:S(2)}) collective-permute-start(bf16[2,256,4,128]{3,1,2,0:T(8,128)(2,1)S(1)} %pad_maximum_fusion), channel_id=1, source_target_pairs={{0,3},{1,4},{2,5},{3,6},{4,7},{8,11},{9,12},{10,13},{11,14},{12,15... | collective-permute-start | bytes 1572872 | tf_op jit(solution)/shard_map/ppermute | solution.py:14
  17.7 55.9 %collective-permute-start.2 = (bf16[2,256,4,128]{3,1,2,0:T(8,128)(2,1)S(1)}, bf16[2,256,4,128]{3,1,2,0:T(8,128)(2,1)}, u32[]{:S(2)}, u32[]{:S(2)}) collective-permute-start(bf16[2,256,4,128]{3,1,2,0:T(8,128)(2,1)S(1)} %pad_maximum_fusion), channel_id=1, source_target_pairs={{0,2},{1,3},{2,4},{3,5},{4,6},{5,7},{8,10},{9,11},{10,12},{11,13},... | collective-permute-start | bytes 1572872 | tf_op jit(solution)/shard_map/ppermute | solution.py:14
  19.8 87.7 %collective-permute-start.3 = (bf16[2,256,4,128]{3,1,2,0:T(8,128)(2,1)S(1)}, bf16[2,256,4,128]{3,1,2,0:T(8,128)(2,1)}, u32[]{:S(2)}, u32[]{:S(2)}) collective-permute-start(bf16[2,256,4,128]{3,1,2,0:T(8,128)(2,1)S(1)} %pad_maximum_fusion), channel_id=1, source_target_pairs={{0,1},{1,2},{2,3},{3,4},{4,5},{5,6},{6,7},{8,9},{9,10},{10,11},{11... | collective-permute-start | bytes 1572872 | tf_op jit(solution)/shard_map/ppermute | solution.py:14
  111.7 7.0 copy-start
Sparse Core Ops, SparseCore 0:
  8.9 652.1 all-gather.1
  677.7 52.5 reduce-scatter.1
where the time goes:
time: 740 us; the launch traced here: 737 us
  waiting for transfers between devices  666 us (90%)
  matrix products  30 us (4%)
  starting transfers between devices  15 us (2%)
  between operations  13.5 us (2%)
  local copies, waits for them, and re-layouts  9.19 us (1%)
    all_gather x1, waiting for transfers between devices, on_device(): piece = lax.all_gather(output_projection_weight, 'srv', axis=2, tiled=True)  532 us
    ppermute x4, waiting for transfers between devices, from_behind(): return lax.ppermute(block, axis, route)  80.5 us
    reduce_scatter x1, waiting for transfers between devices, on_device(): lax.psum_scatter(partial_sum.astype(jnp.bfloat16), ('grp', 'kv'), scatter...  52.7 us
    dot_general x1, matrix products, on_device(): jnp.dot(attention_output, piece.reshape(inner, piece.shape[2]), preferred...  16.5 us
    ppermute x4, starting transfers between devices, from_behind(): return lax.ppermute(block, axis, route)  14.9 us
  transfers between devices with their start and end apart: 6, of which 6 were waited for; matrix products, arithmetic and copies ran while one was open for 3% of the time, Pallas kernels for 0%

commit v1 on v0

--- a/solution.py
+++ b/solution.py
@@ -58,14 +58,34 @@
     key_pos = (shard - REACH) * token_count + jnp.arange(window.shape[1], dtype=jnp.int32)
     attention_output = attend(queries, window[0], window[1], query_pos, key_pos, lengths)
     inner = attention_output.shape[1]
-    piece = lax.all_gather(output_projection_weight, "srv", axis=2, tiled=True)
-    partial_sum = jnp.dot(
-        attention_output, piece.reshape(inner, piece.shape[2]), preferred_element_type=jnp.float32
+    weight = output_projection_weight.reshape(inner, output_projection_weight.shape[2])
+    everyone = lax.all_gather(attention_output, "srv", axis=0, tiled=True)
+    partial_sum = jnp.dot(everyone, weight, preferred_element_type=jnp.float32)
+    summed = lax.psum_scatter(
+        partial_sum.astype(jnp.bfloat16), ("grp", "kv"), scatter_dimension=0, tiled=True
     )
-    summed = lax.psum_scatter(
-        partial_sum.astype(jnp.bfloat16), ("grp", "kv"), scatter_dimension=1, tiled=True
-    )
-    return summed
+    return to_token_owners(summed, token_count)
+
+
+def to_token_owners(summed, token_count):
+    shards = lax.axis_size("srv")
+    blocks = lax.axis_size("grp") * lax.axis_size("kv")
+    per = shards // blocks
+    width = summed.shape[1]
+    mine = lax.axis_index("srv") % per
+    out = jnp.zeros((token_count, per * width), summed.dtype)
+    for shift in range(per):
+        route = []
+        for block in range(blocks):
+            for shard in range(shards):
+                to = block * per + (shard % per + shift) % per
+                route.append((block * shards + shard, (shard // per) * shards + to))
+        leaving = lax.dynamic_slice_in_dim(
+            summed, ((mine + shift) % per) * token_count, token_count, 0
+        )
+        came = lax.ppermute(leaving, ("grp", "kv", "srv"), route)
+        out = lax.dynamic_update_slice_in_dim(out, came, ((mine - shift) % per) * width, 1)
+    return out
 
 
 def solution(mesh):

time: 740 us -> 334 us (0.45)
  the two profiles are of different devices: /device:TPU:3 before, /device:TPU:2 now
where the time goes in v1:
time: 334 us; the launch traced here: 333 us
  waiting for transfers between devices  255 us (76%)
  matrix products  28.4 us (9%)
  starting transfers between devices  20.4 us (6%)
  between operations  13.6 us (4%)
  local copies, waits for them, and re-layouts  11.1 us (3%)
  other arithmetic  5.04 us (2%)
    all_gather x1, waiting for transfers between devices, on_device(): everyone = lax.all_gather(attention_output, 'srv', axis=0, tiled=True)  159 us
    reduce_scatter x1, waiting for transfers between devices, on_device(): lax.psum_scatter(partial_sum.astype(jnp.bfloat16), ('grp', 'kv'), scatter...  41.7 us
    ppermute x2, waiting for transfers between devices, to_token_owners(): came = lax.ppermute(leaving, ('grp', 'kv', 'srv'), route)  35 us
    ppermute x4, waiting for transfers between devices, from_behind(): return lax.ppermute(block, axis, route)  18.4 us
    ppermute x4, starting transfers between devices, from_behind(): return lax.ppermute(block, axis, route)  14.2 us
    dot_general x1, matrix products, on_device(): partial_sum = jnp.dot(everyone, weight, preferred_element_type=jnp.float32)  14 us
    dot_general x1, matrix products, attend(): jnp.einsum('jhtw,wjd->tjhd', weights.astype(jnp.bfloat16), window_values,...  11.4 us
  transfers between devices with their start and end apart: 8, of which 6 were waited for; matrix products, arithmetic and copies ran while one was open for 2% of the time, Pallas kernels for 0%

profile of v1, /device:TPU:2, one launch (start us, length us, event | category | flops | bytes accessed | tf_op | source)
XLA Modules:
  0.0 333.1 jit_solution(11114876444853644835)
XLA Ops:
  6.5 1.1 copy_bitcast_fusion
  7.7 5.3 %collective-permute-start = (bf16[2,256,4,128]{3,1,2,0:T(8,128)(2,1)S(1)}, bf16[2,256,4,128]{3,1,2,0:T(8,128)(2,1)}, u32[]{:S(2)}, u32[]{:S(2)}) collective-permute-start(bf16[2,256,4,128]{3,1,2,0:T(8,128)(2,1)S(1)} %pad_maximum_fusion), channel_id=1, source_target_pairs={{0,4},{1,5},{2,6},{3,7},{8,12},{9,13},{10,14},{11,15},{16,20},{17,... | collective-permute-start | bytes 1572872 | tf_op jit(solution)/shard_map/ppermute | solution.py:14
  13.0 5.2 %collective-permute-start.1 = (bf16[2,256,4,128]{3,1,2,0:T(8,128)(2,1)S(1)}, bf16[2,256,4,128]{3,1,2,0:T(8,128)(2,1)}, u32[]{:S(2)}, u32[]{:S(2)}) collective-permute-start(bf16[2,256,4,128]{3,1,2,0:T(8,128)(2,1)S(1)} %pad_maximum_fusion), channel_id=1, source_target_pairs={{0,3},{1,4},{2,5},{3,6},{4,7},{8,11},{9,12},{10,13},{11,14},{12,15... | collective-permute-start | bytes 1572872 | tf_op jit(solution)/shard_map/ppermute | solution.py:14
  18.2 1.3 collective-permute-start.2
  19.5 2.3 collective-permute-start.3
  21.9 0.8 reduce-window.9
  22.7 0.7 bitcast_subtract_fusion
  23.4 0.1 select_reduce_fusion
  23.5 0.3 compare_and_fusion
  23.8 1.5 reshape.102
  25.3 1.1 constant_dynamic-update-slice_fusion.4
  26.4 9.4 %collective-permute-done.1 = bf16[2,256,4,128]{3,1,2,0:T(8,128)(2,1)} collective-permute-done((bf16[2,256,4,128]{3,1,2,0:T(8,128)(2,1)S(1)}, bf16[2,256,4,128]{3,1,2,0:T(8,128)(2,1)}, u32[]{:S(2)}, u32[]{:S(2)}) %collective-permute-start.1) | collective-permute-done | bytes 524320 | tf_op jit(solution)/shard_map/ppermute | solution.py:14
  35.8 1.1 constant_dynamic-update-slice_fusion.3
  36.9 9.0 %collective-permute-done.2 = bf16[2,256,4,128]{3,1,2,0:T(8,128)(2,1)S(1)} collective-permute-done((bf16[2,256,4,128]{3,1,2,0:T(8,128)(2,1)S(1)}, bf16[2,256,4,128]{3,1,2,0:T(8,128)(2,1)S(1)}, u32[]{:S(2)}, u32[]{:S(2)}) %collective-permute-start.2) | collective-permute-done | bytes 524320 | tf_op jit(solution)/shard_map/ppermute | solution.py:14
  45.9 0.1 constant_dynamic-update-slice_fusion.2
  46.0 0.1 constant_dynamic-update-slice_fusion.1
  46.1 0.1 constant_dynamic-update-slice_fusion
  46.2 3.1 fusion.9
  49.3 3.0 fusion
  52.3 3.9 %copy-done = f32[4,4,256,1280]{2,3,1,0:T(8,128)} copy-done((f32[4,4,256,1280]{2,3,1,0:T(8,128)}, f32[4,4,256,1280]{2,3,1,0:T(8,128)S(1)}, u32[]{:S(2)}) %copy-start) | copy-done | bytes 20971544
  56.2 11.4 %fusion.5 = bf16[256,4,4,128]{0,3,2,1:T(8,128)(2,1)} fusion(f32[4,4,256,1280]{2,3,1,0:T(8,128)} %copy-done, f32[4,4,256]{2,1,0:T(4,128)S(1)} %get-tuple-element.7, bf16[2,1280,4,128]{3,1,2,0:T(8,128)(2,1)S(1)} %constant_dynamic-update-slice_fusion, f32[256,4,4]{0,2,1:T(4,128)S(1)} %bitcast.34), kind=kOutput, calls=%fused_computation.8 | convolution fusion | flops 1353711616 | bytes 23363584 | tf_op jit(solution)/shard_map/jhtw,wjd->tjhd/dot_general | solution.py:39
  67.6 0.2 reduce-scatter.2.cloned.1.call-start
  67.8 159.5 %all-gather.2.cloned.1.call-done = bf16[2048,2048]{0,1:T(8,128)(2,1)} async-done(((bf16[256,2048]{0,1:T(8,128)(2,1)}), bf16[2048,2048]{0,1:T(8,128)(2,1)}) %all-gather.2.cloned.1.call-update) | async-done | bytes 8388624 | tf_op jit(solution)/shard_map/all_gather | solution.py:62
  227.3 14.0 %convolution_convert_fusion = bf16[2048,1024]{1,0:T(8,128)(2,1)} fusion(bf16[2048,2048]{0,1:T(8,128)(2,1)} %all-gather.2.cloned.1.call-done, bf16[2048,1024]{1,0:T(8,128)(2,1)} %bitcast.35), kind=kOutput, calls=%fused_computation.6 | convolution fusion | flops 8592031744 | bytes 16777216 | tf_op jit(solution)/shard_map/dot_general | solution.py:63
  241.3 41.7 %reduce-scatter.2.cloned.1.call-done = bf16[512,1024]{1,0:T(8,128)(2,1)} async-done(((bf16[2048,1024]{1,0:T(8,128)(2,1)}), bf16[512,1024]{1,0:T(8,128)(2,1)}) %reduce-scatter.2.cloned.1.call-update) | async-done | bytes 1048592 | tf_op jit(solution)/shard_map/reduce_scatter | solution.py:64
  283.0 1.3 constant_dynamic-slice_fusion
  284.3 4.5 %collective-permute-start.4 = (bf16[256,1024]{1,0:T(8,128)(2,1)S(1)}, bf16[256,1024]{1,0:T(8,128)(2,1)S(1)}, u32[]{:S(2)}, u32[]{:S(2)}) collective-permute-start(bf16[256,1024]{1,0:T(8,128)(2,1)S(1)} %get-tuple-element.6), channel_id=1, source_target_pairs={{0,0},{1,1},{2,8},{3,9},{4,16},{5,17},{6,24},{7,25},{8,2},{9,3},{1... | collective-permute-start | bytes 1572872 | tf_op jit(solution)/shard_map/ppermute | solution.py:86
  288.8 1.5 collective-permute-start.5
  290.3 28.4 %collective-permute-done.4 = bf16[256,1024]{1,0:T(8,128)(2,1)S(1)} collective-permute-done((bf16[256,1024]{1,0:T(8,128)(2,1)S(1)}, bf16[256,1024]{1,0:T(8,128)(2,1)S(1)}, u32[]{:S(2)}, u32[]{:S(2)}) %collective-permute-start.4) | collective-permute-done | bytes 524320 | tf_op jit(solution)/shard_map/ppermute | solution.py:86
  318.7 0.1 broadcast_in_dim.20
  318.9 6.6 %collective-permute-done.5 = bf16[256,1024]{1,0:T(8,128)(2,1)S(1)} collective-permute-done((bf16[256,1024]{1,0:T(8,128)(2,1)S(1)}, bf16[256,1024]{1,0:T(8,128)(2,1)S(1)}, u32[]{:S(2)}, u32[]{:S(2)}) %collective-permute-start.5) | collective-permute-done | bytes 524320 | tf_op jit(solution)/shard_map/ppermute | solution.py:86
  325.5 0.8 constant_dynamic-update-slice_fusion.5
  (12 shorter events, 0.2 us)
Async XLA Ops:
  6.5 220.8 %all-gather.2.cloned.1.call-start = ((), (), s32[]{:S(2)}) async-start(), calls=%async_computation.1 | async-start | bytes 9437184 | tf_op jit(solution)/shard_map/all_gather | solution.py:62
  7.7 17.6 %collective-permute-start = (bf16[2,256,4,128]{3,1,2,0:T(8,128)(2,1)S(1)}, bf16[2,256,4,128]{3,1,2,0:T(8,128)(2,1)}, u32[]{:S(2)}, u32[]{:S(2)}) collective-permute-start(bf16[2,256,4,128]{3,1,2,0:T(8,128)(2,1)S(1)} %pad_maximum_fusion), channel_id=1, source_target_pairs={{0,4},{1,5},{2,6},{3,7},{8,12},{9,13},{10,14},{11,15},{16,20},{17,... | collective-permute-start | bytes 1572872 | tf_op jit(solution)/shard_map/ppermute | solution.py:14
  13.0 22.8 %collective-permute-start.1 = (bf16[2,256,4,128]{3,1,2,0:T(8,128)(2,1)S(1)}, bf16[2,256,4,128]{3,1,2,0:T(8,128)(2,1)}, u32[]{:S(2)}, u32[]{:S(2)}) collective-permute-start(bf16[2,256,4,128]{3,1,2,0:T(8,128)(2,1)S(1)} %pad_maximum_fusion), channel_id=1, source_target_pairs={{0,3},{1,4},{2,5},{3,6},{4,7},{8,11},{9,12},{10,13},{11,14},{12,15... | collective-permute-start | bytes 1572872 | tf_op jit(solution)/shard_map/ppermute | solution.py:14
  18.2 27.7 %collective-permute-start.2 = (bf16[2,256,4,128]{3,1,2,0:T(8,128)(2,1)S(1)}, bf16[2,256,4,128]{3,1,2,0:T(8,128)(2,1)S(1)}, u32[]{:S(2)}, u32[]{:S(2)}) collective-permute-start(bf16[2,256,4,128]{3,1,2,0:T(8,128)(2,1)S(1)} %pad_maximum_fusion), channel_id=1, source_target_pairs={{0,2},{1,3},{2,4},{3,5},{4,6},{5,7},{8,10},{9,11},{10,12},{11,13},... | collective-permute-start | bytes 1572872 | tf_op jit(solution)/shard_map/ppermute | solution.py:14
  19.5 26.5 %collective-permute-start.3 = (bf16[2,256,4,128]{3,1,2,0:T(8,128)(2,1)S(1)}, bf16[2,256,4,128]{3,1,2,0:T(8,128)(2,1)S(1)}, u32[]{:S(2)}, u32[]{:S(2)}) collective-permute-start(bf16[2,256,4,128]{3,1,2,0:T(8,128)(2,1)S(1)} %pad_maximum_fusion), channel_id=1, source_target_pairs={{0,1},{1,2},{2,3},{3,4},{4,5},{5,6},{6,7},{8,9},{9,10},{10,11},{11... | collective-permute-start | bytes 1572872 | tf_op jit(solution)/shard_map/ppermute | solution.py:14
  49.3 7.0 %copy-start = (f32[4,4,256,1280]{2,3,1,0:T(8,128)}, f32[4,4,256,1280]{2,3,1,0:T(8,128)S(1)}, u32[]{:S(2)}) copy-start(f32[4,4,256,1280]{2,3,1,0:T(8,128)S(1)} %get-tuple-element.8) | copy-start | bytes 62914564
  67.6 215.4 %reduce-scatter.2.cloned.1.call-start = ((), (), s32[]{:S(2)}) async-start(), calls=%async_computation.2 | async-start | bytes 5242880 | tf_op jit(solution)/shard_map/reduce_scatter | solution.py:64
  284.3 34.4 %collective-permute-start.4 = (bf16[256,1024]{1,0:T(8,128)(2,1)S(1)}, bf16[256,1024]{1,0:T(8,128)(2,1)S(1)}, u32[]{:S(2)}, u32[]{:S(2)}) collective-permute-start(bf16[256,1024]{1,0:T(8,128)(2,1)S(1)} %get-tuple-element.6), channel_id=1, source_target_pairs={{0,0},{1,1},{2,8},{3,9},{4,16},{5,17},{6,24},{7,25},{8,2},{9,3},{1... | collective-permute-start | bytes 1572872 | tf_op jit(solution)/shard_map/ppermute | solution.py:86
  288.8 36.7 %collective-permute-start.5 = (bf16[256,1024]{1,0:T(8,128)(2,1)S(1)}, bf16[256,1024]{1,0:T(8,128)(2,1)S(1)}, u32[]{:S(2)}, u32[]{:S(2)}) collective-permute-start(bf16[256,1024]{1,0:T(8,128)(2,1)S(1)} %get-tuple-element.5), channel_id=1, source_target_pairs={{0,1},{1,0},{2,9},{3,8},{4,17},{5,16},{6,25},{7,24},{8,3},{9,2},{1... | collective-permute-start | bytes 1572872 | tf_op jit(solution)/shard_map/ppermute | solution.py:86
  318.9 6.6 %copy-start.1 = (bf16[256,2048]{1,0:T(8,128)(2,1)}, bf16[256,2048]{1,0:T(8,128)(2,1)S(1)}, u32[]{:S(2)}) copy-start(bf16[256,2048]{1,0:T(8,128)(2,1)S(1)} %constant_dynamic-update-slice_fusion.6) | copy-start | bytes 3145732
Sparse Core Ops, SparseCore 0:
  67.7 159.5 all-gather.1
  241.4 41.5 reduce-scatter.1

commit v2 on v0

v2 whole, which is shorter than its diff:
```python
import functools
import math

import jax
import jax.numpy as jnp
from jax import lax
from jax.experimental import pallas as pl
from jax.experimental.pallas import tpu as pltpu
from jax.sharding import PartitionSpec as P

REACH = 4
PIECES = 4
FAR = -1e30
MESH = pl.DeviceIdType.MESH


def layer(plan, lengths, q_ref, kv_ref, w_ref, out_ref, kvw, bias, abuf, wbuf, send1, recv1,
          acc, send2, recv2, send3, kv_s, kv_r, y_s, y_r, swap_s, swap_r, own_w, w_s, w_r,
          a_s, a_r, s1, r1, s2, r2, s3, r3):
    head, halves, lanes, pairs, chunk, own_chunks = plan
    tokens, inner = q_ref.shape
    groups = kvw.shape[3] // head
    heads = inner // (groups * head)
    span = heads * head
    chunks = wbuf.shape[0]
    columns = w_ref.shape[1]
    rows = halves * tokens
    a, g, s = lax.axis_index("grp"), lax.axis_index("kv"), lax.axis_index("srv")
    u, v = s // pairs, s % pairs
    q = a * halves + g

    core = (1 - a, g, s)
    beside = (a, g, u * pairs + 1 - v)
    ahead = (a, g, s + pairs)
    behind = (a, g, s - pairs)
    across = (u // halves, u % halves, q * pairs + v)
    away = q != u
    right, left = u + 1 < lanes, u > 0

    def other_half(k):
        return (a, (g + k) % halves, s)

    barrier = pltpu.get_barrier_semaphore()

    def greet(device):
        pl.semaphore_signal(barrier, inc=1, device_id=device, device_id_type=MESH)

    greet(core)
    greet(beside)
    for k in range(1, halves):
        greet(other_half(k))
    pl.when(right)(lambda: greet(ahead))
    pl.when(left)(lambda: greet(behind))
    pl.when(away)(lambda: greet(across))
    peers = jnp.int32(1 + halves)
    for there in (right, left, away):
        peers = peers + jnp.where(there, 1, 0)
    pl.semaphore_wait(barrier, peers)

    def remote(src, dst, send, recv, device):
        return pltpu.make_async_remote_copy(
            src_ref=src, dst_ref=dst, send_sem=send, recv_sem=recv,
            device_id=device, device_id_type=MESH,
        )

    def hop(d):
        src = kv_ref.at[a] if d == 2 else kvw.at[a, 2]
        return remote(src, kvw.at[a, d], kv_s.at[d // 2 - 1], kv_r.at[d // 2 - 1], ahead)

    def sideways(d):
        src = kv_ref.at[a] if d == 0 else kvw.at[a, d]
        slot = jnp.where(v == 0, d + 1, d - 1)
        return remote(src, kvw.at[a, slot], y_s.at[d // 2], y_r.at[slot // 2], beside)

    def came(d):
        return remote(kv_ref.at[a], kvw.at[a, d], y_s.at[0], y_r.at[d // 2], beside)

    def swap(d):
        return remote(kvw.at[a, d], kvw.at[a, d], swap_s.at[d - 1], swap_r.at[d - 1], core)

    def swapped(d):
        return remote(kvw.at[a, d], kvw.at[1 - a, d], swap_s.at[d - 1], swap_r.at[d - 1], core)

    depth = inner // PIECES

    def weight(c, p):
        part = pl.ds(p * depth, depth)
        return remote(
            w_ref.at[part, pl.ds(c * chunk, chunk)], wbuf.at[own_chunks + c, part],
            w_s.at[c, p], w_r.at[c, p], beside,
        )

    def own_weight(c):
        return pltpu.make_async_copy(
            w_ref.at[:, pl.ds(c * chunk, chunk)], wbuf.at[c], own_w.at[c]
        )

    two, four = u >= 1, u >= 2
    pl.when(right)(lambda: hop(2).start())
    pl.when(v == 0)(lambda: sideways(0).start())
    weight(0, 0).start()
    for c in range(own_chunks):
        own_weight(c).start()
    kvw[0, 0] = kv_ref[0]
    kvw[1, 0] = kv_ref[1]
    for d in range(1, REACH + 1):
        @pl.when(s < d)
        def _():
            kvw[0, d] = jnp.zeros(kvw.shape[2:], kvw.dtype)
            kvw[1, d] = jnp.zeros(kvw.shape[2:], kvw.dtype)

    row = lax.broadcasted_iota(jnp.int32, (tokens, 1), 0)
    query_pos = s * tokens + row
    first = jnp.zeros((tokens, 1), jnp.int32)
    start = jnp.int32(0)
    for i in range(lengths.shape[0]):
        first = jnp.where(query_pos >= start, start, first)
        start = start + lengths[i]
    lane = lax.broadcasted_iota(jnp.int32, (tokens, tokens), 1)
    for d in range(REACH + 1):
        key_pos = (s - d) * tokens + lane
        allowed = (key_pos >= first) & (key_pos <= query_pos)
        bias[:, d * tokens:(d + 1) * tokens] = jnp.where(allowed, 0.0, FAR)

    @pl.when(two)
    def _():
        hop(2).wait_recv()
        pl.when(right)(lambda: hop(4).start())
        sideways(2).start()
        swap(2).start()

    weight(0, 1).start()

    @pl.when(s >= 1)
    def _():
        came(1).wait_recv()
        swap(1).start()

    @pl.when(four)
    def _():
        hop(4).wait_recv()
        pl.when(v == 1)(lambda: sideways(4).start())
        swap(4).start()

    for p in range(2, PIECES):
        weight(0, p).start()
    for c in range(1, own_chunks):
        for p in range(PIECES):
            weight(c, p).start()

    @pl.when(s >= 3)
    def _():
        came(3).wait_recv()
        swap(3).start()

    for d in range(1, REACH + 1):
        pl.when(s >= d)(lambda d=d: swapped(d).wait_recv())

    def relay(way, d, j):
        block = u - (d - 1) if way == 0 else u + (d - 1)
        part = abuf.at[block, :, pl.ds(pl.multiple_of(j * span, span), span)]
        return remote(part, part, a_s.at[way, d - 1, j], a_r.at[way, d - 1, j],
                      ahead if way == 0 else behind)

    def relayed(way, d, j):
        block = u - d if way == 0 else u + d
        part = abuf.at[block, :, pl.ds(pl.multiple_of(j * span, span), span)]
        return remote(part, part, a_s.at[way, d - 1, j], a_r.at[way, d - 1, j],
                      behind if way == 0 else ahead)

    def holds(way, d):
        return u >= d if way == 0 else u + d < lanes

    def may_send(way):
        return right if way == 0 else left

    def forward(d, j):
        for way in range(2):
            @pl.when(holds(way, d - 1))
            def _():
                relayed(way, d - 1, j).wait_recv()
                pl.when(may_send(way))(lambda: relay(way, d, j).start())

    factor = math.log2(math.e) / math.sqrt(head)

    def per_group(j, carry):
        at = pl.ds(pl.multiple_of(j * head, head), head)

        def per_head(h, inside):
            mine = pl.ds(pl.multiple_of(j * span + h * head, head), head)
            window = kvw[0, :, :, at].reshape((REACH + 1) * tokens, head)
            scores = lax.dot_general(
                q_ref[:, mine], window, (((1,), (1,)), ((), ())),
                preferred_element_type=jnp.float32,
            ) + bias[...]
            peak = jnp.max(scores, axis=1, keepdims=True)
            weights = jnp.exp2((scores - peak) * factor)
            total = jnp.sum(weights, axis=1, keepdims=True)
            numer = jnp.dot(
                weights.astype(jnp.bfloat16),
                kvw[1, :, :, at].reshape((REACH + 1) * tokens, head),
                preferred_element_type=jnp.float32,
            )
            abuf[u, :, mine] = (numer / total).astype(abuf.dtype)
            return inside

        lax.fori_loop(0, heads, per_head, 0)
        for way in range(2):
            pl.when(may_send(way))(lambda: relay(way, 1, j).start())
        pl.when(j >= 2)(lambda: forward(2, j - 2))
        return carry

    lax.fori_loop(0, groups, per_group, 0)

    def over_groups(low, body):
        def step(j, carry):
            body(j)
            return carry

        lax.fori_loop(low, groups, step, 0)

    over_groups(max(0, groups - 2), lambda j: forward(2, j))
    for d in range(3, lanes):
        over_groups(0, lambda j: forward(d, j))

    def last(j):
        for way in range(2):
            pl.when(holds(way, lanes - 1))(lambda: relayed(way, lanes - 1, j).wait_recv())

    over_groups(0, last)

    def to_core(c):
        return remote(send1.at[c], recv1.at[c], s1.at[c], r1.at[c], core)

    def to_half(c, k):
        return remote(send2.at[c, pl.ds((g + k) % halves * tokens, tokens)], recv2.at[c, k - 1],
                      s2.at[c, k - 1], r2.at[c, k - 1], other_half(k))

    def result(c):
        own = c < own_chunks
        offset = jnp.where(own, v * columns + c * chunk,
                           (1 - v) * columns + (c - own_chunks) * chunk)
        return out_ref.at[:, pl.ds(pl.multiple_of(offset, chunk), chunk)]

    def to_owner(c):
        return remote(send3.at[c], result(c), s3.at[c], r3.at[c], across)

    def to_self(c):
        return pltpu.make_async_copy(send3.at[c], result(c), r3.at[c])

    def product(half, c):
        left_side = abuf[pl.ds(half * halves, halves)].reshape(rows, inner)
        return jnp.dot(left_side, wbuf[c], preferred_element_type=jnp.float32)

    def second(c):
        for k in range(1, halves):
            to_half(c, k).wait_recv()
        total = acc[c, pl.ds(g * tokens, tokens)]
        for k in range(1, halves):
            total = total + recv2[c, k - 1].astype(jnp.float32)
        send3[c] = total.astype(send3.dtype)
        pl.when(away)(lambda: to_owner(c).start())
        pl.when(jnp.logical_not(away))(lambda: to_self(c).start())

    def per_chunk(c, carry):
        pl.when(c < own_chunks)(lambda: own_weight(c).wait())

        @pl.when(c >= own_chunks)
        def _():
            for p in range(PIECES):
                weight(c - own_chunks, p).wait_recv()

        send1[c] = product(1 - a, c).astype(send1.dtype)
        to_core(c).start()
        acc[c] = product(a, c)
        pl.when(c >= 1)(lambda: second(c - 1))
        to_core(c).wait_recv()
        total = acc[c] + recv1[c].astype(jnp.float32)
        acc[c] = total
        send2[c] = total.astype(send2.dtype)
        for k in range(1, halves):
            to_half(c, k).start()
        return carry

    lax.fori_loop(0, chunks, per_chunk, 0)
    second(chunks - 1)

    pl.when(right)(lambda: hop(2).wait_send())
    pl.when(two & right)(lambda: hop(4).wait_send())
    pl.when(v == 0)(lambda: sideways(0).wait_send())
    pl.when(two)(lambda: sideways(2).wait_send())
    pl.when(four & (v == 1))(lambda: sideways(4).wait_send())
    for d in range(1, REACH + 1):
        pl.when(s >= d)(lambda d=d: swap(d).wait_send())
    for c in range(own_chunks):
        for p in range(PIECES):
            weight(c, p).wait_send()
    for d in range(1, lanes):
        for way in range(2):
            @pl.when(holds(way, d - 1) & may_send(way))
            def _():
                over_groups(0, lambda j: relay(way, d, j).wait_send())

    def finish(c, carry):
        to_core(c).wait_send()
        for k in range(1, halves):
            to_half(c, k).wait_send()

        @pl.when(away)
        def _():
            to_owner(c).wait_send()
            to_owner(c).wait_recv()

        pl.when(jnp.logical_not(away))(lambda: to_self(c).wait())
        return carry

    lax.fori_loop(0, chunks, finish, 0)


def on_device(queries, keys, values, lengths, output_projection_weight):
    tokens = queries.shape[0]
    cores, halves = lax.axis_size("grp"), lax.axis_size("kv")
    lanes = cores * halves
    pairs = lax.axis_size("srv") // lanes
    assert cores == 2 and pairs == 2
    q = queries.reshape(tokens, -1)
    inner = q.shape[1]
    kv = jnp.stack([keys.reshape(tokens, -1), values.reshape(tokens, -1)])
    weight = output_projection_weight.reshape(inner, -1)
    columns = weight.shape[1]
    chunk = max(128, columns // 4)
    own_chunks = columns // chunk
    chunks = own_chunks * pairs
    groups, head = keys.shape[1], keys.shape[2]
    rows = halves * tokens
    dma = pltpu.SemaphoreType.DMA
    bf16, f32 = jnp.bfloat16, jnp.float32
    vmem = pl.BlockSpec(memory_space=pltpu.VMEM)
    return pl.pallas_call(
        functools.partial(layer, (head, halves, lanes, pairs, chunk, own_chunks)),
        out_shape=jax.ShapeDtypeStruct((tokens, pairs * columns), bf16),
        in_specs=[
            pl.BlockSpec(memory_space=pltpu.SMEM), vmem, vmem,
            pl.BlockSpec(memory_space=pl.ANY),
        ],
        out_specs=pl.BlockSpec(memory_space=pl.ANY),
        scratch_shapes=[
            pltpu.VMEM((2, REACH + 1, tokens, kv.shape[2]), bf16),
            pltpu.VMEM((tokens, (REACH + 1) * tokens), f32),
            pltpu.VMEM((lanes, tokens, inner), bf16),
            pltpu.VMEM((chunks, inner, chunk), bf16),
            pltpu.VMEM((chunks, rows, chunk), bf16),
            pltpu.VMEM((chunks, rows, chunk), bf16),
            pltpu.VMEM((chunks, rows, chunk), f32),
            pltpu.VMEM((chunks, rows, chunk), bf16),
            pltpu.VMEM((chunks, halves - 1, tokens, chunk), bf16),
            pltpu.VMEM((chunks, tokens, chunk), bf16),
            dma((2,)), dma((2,)), dma((3,)), dma((2,)), dma((REACH,)), dma((REACH,)),
            dma((own_chunks,)), dma((own_chunks, PIECES)), dma((own_chunks, PIECES)),
            dma((2, lanes - 1, groups)), dma((2, lanes - 1, groups)),
            dma((chunks,)), dma((chunks,)),
            dma((chunks, halves - 1)), dma((chunks, halves - 1)),
            dma((chunks,)), dma((chunks,)),
        ],
        compiler_params=pltpu.CompilerParams(
            collective_id=0, has_side_effects=True, vmem_limit_bytes=60 * 1024 * 1024
        ),
    )(lengths, q, kv, weight)


def solution(mesh):
    placed = (
        P("srv", "kv", "grp"),
        P("srv", "kv", None),
        P("srv", "kv", None),
        P(),
        P("kv", "grp", "srv"),
    )
    return jax.shard_map(
        on_device, mesh=mesh, in_specs=placed, out_specs=P("srv", ("grp", "kv")), check_vma=False
    )
```

time: 740 us -> 177 us (0.24)
  waiting for transfers between devices: 666 us -> 0 us
  Pallas kernels: 0 us -> 169 us
  matrix products: 30 us -> 0 us
  starting transfers between devices: 15 us -> 0 us
  between operations: 13.5 us -> 0.02 us
    all_gather x1 -> x0, waiting for transfers between devices: 532 us -> none  [on_device(): piece = lax.all_gather(output_projection_weight, 'srv', axis=2, tiled=True)]
    pallas_call x0 -> x1, Pallas kernels: none -> 169 us  [on_device(): pl.pallas_call(functools.partial(layer, (head, halves, lanes, pairs, chun...]
    ppermute x4 -> x0, waiting for transfers between devices: 80.5 us -> none  [from_behind(): return lax.ppermute(block, axis, route)]
    reduce_scatter x1 -> x0, waiting for transfers between devices: 52.7 us -> none  [on_device(): lax.psum_scatter(partial_sum.astype(jnp.bfloat16), ('grp', 'kv'), scatter...]
    dot_general x3 -> x0, matrix products: 30 us -> none  [the longest x1 16.5 us: on_device(): jnp.dot(attention_output, piece.reshape(inner, piece.shape[2]), preferred...]
    ppermute x4 -> x0, starting transfers between devices: 14.9 us -> none  [from_behind(): return lax.ppermute(block, axis, route)]
  transfers between devices with their start and end apart: 6 -> 0, of which waited for: 6 -> 0; matrix products, arithmetic and copies ran while one was open for 3% -> 0% of each run, Pallas kernels for 0% -> 0%
where the time goes in v2:
time: 177 us
  Pallas kernels  169 us (95%)
  local copies, waits for them, and re-layouts  6.88 us (4%)
    pallas_call x1, Pallas kernels, on_device(): pl.pallas_call(functools.partial(layer, (head, halves, lanes, pairs, chun...  169 us
    unnamed x2, local copies, waits for them, and re-layouts  4.78 us

profile of v2, /device:TPU:3, one launch (start us, length us, event | category | flops | bytes accessed | tf_op | source)
XLA Modules:
  0.0 177.1 jit_solution(10129911300932515679)
XLA Ops:
  0.0 1.1 stack_reshape.6
  1.1 1.1 stack_reshape.7
  2.1 0.9 pad_maximum_fusion.kv_ref
  3.0 2.5 %copy.6 = bf16[32,8,4,512]{3,1,2,0:T(8,128)(2,1)} copy(bf16[32,8,4,512]{3,2,1,0:T(4,128)(2,1)} %bitcast.5) | data formatting | bytes 2097152
  5.4 169.3 %shard_map.55 = bf16[256,2048]{1,0:T(8,128)(2,1)} custom-call(s32[4]{0:T(128)} %lengths.1, bf16[256,2048]{1,0:T(8,128)(2,1)} %bitcast.4, bf16[2,256,512]{2,1,0:T(8,128)(2,1)} %pad_maximum_fusion.kv_ref, bf16[2048,1024]{1,0:T(8,128)(2,1)} %bitcast.3), custom_call_target="tpu_custom_call" | custom-call | tf_op jit(solution)/shard_map/pallas_call | solution.py:339
  174.8 2.3 %copy.8 = bf16[256,2048]{1,0:T(8,128)(2,1)} copy(bf16[256,2048]{1,0:T(8,128)(2,1)} %shard_map.55) | data formatting | bytes 2097152

commit v3 on v2

--- a/solution.py
+++ b/solution.py
@@ -273,17 +273,22 @@
         send1[c] = product(1 - a, c).astype(send1.dtype)
         to_core(c).start()
         acc[c] = product(a, c)
-        pl.when(c >= 1)(lambda: second(c - 1))
+        pl.when(c >= 1)(lambda: merge(c - 1))
+        pl.when(c >= 3)(lambda: second(c - 3))
+        return carry
+
+    def merge(c):
         to_core(c).wait_recv()
         total = acc[c] + recv1[c].astype(jnp.float32)
         acc[c] = total
         send2[c] = total.astype(send2.dtype)
         for k in range(1, halves):
             to_half(c, k).start()
-        return carry
 
     lax.fori_loop(0, chunks, per_chunk, 0)
-    second(chunks - 1)
+    merge(chunks - 1)
+    for c in range(max(0, chunks - 3), chunks):
+        second(c)
 
     pl.when(right)(lambda: hop(2).wait_send())
     pl.when(two & right)(lambda: hop(4).wait_send())

time: 177 us -> 178 us (level)
  no operation moved by 1% of the time
where the time goes in v3:
time: 178 us; the launch traced here: 177 us
  Pallas kernels  170 us (96%)
  local copies, waits for them, and re-layouts  6.88 us (4%)
    pallas_call x1, Pallas kernels, on_device(): pl.pallas_call(functools.partial(layer, (head, halves, lanes, pairs, chun...  170 us
    unnamed x2, local copies, waits for them, and re-layouts  4.78 us

profile of v3, /device:TPU:3, one launch (start us, length us, event | category | flops | bytes accessed | tf_op | source)
XLA Modules:
  0.0 177.4 jit_solution(7980145829790498315)
XLA Ops:
  0.0 1.1 stack_reshape.6
  1.1 1.1 stack_reshape.7
  2.1 0.9 pad_maximum_fusion.kv_ref
  3.0 2.5 %copy.6 = bf16[32,8,4,512]{3,1,2,0:T(8,128)(2,1)} copy(bf16[32,8,4,512]{3,2,1,0:T(4,128)(2,1)} %bitcast.5) | data formatting | bytes 2097152
  5.4 169.6 %shard_map.55 = bf16[256,2048]{1,0:T(8,128)(2,1)} custom-call(s32[4]{0:T(128)} %lengths.1, bf16[256,2048]{1,0:T(8,128)(2,1)} %bitcast.4, bf16[2,256,512]{2,1,0:T(8,128)(2,1)} %pad_maximum_fusion.kv_ref, bf16[2048,1024]{1,0:T(8,128)(2,1)} %bitcast.3), custom_call_target="tpu_custom_call" | custom-call | tf_op jit(solution)/shard_map/pallas_call | solution.py:344
  175.1 2.3 %copy.8 = bf16[256,2048]{1,0:T(8,128)(2,1)} copy(bf16[256,2048]{1,0:T(8,128)(2,1)} %shard_map.55) | data formatting | bytes 2097152
